TPU v7x, 32 devices: a whole 2x2x4 slice. The times are simulated.
32 devices in a mesh: dp: 4 (over z), ctx: 4 (over y, core), tensor: 2 (over x).
Axes of the slice: x: 2, y: 2, z: 4, core: 2. Of those that a mesh axis runs over, the one named last changes fastest.
Arguments:
- inputs: bfloat16 [4, 1024, 2048], P('dp', 'ctx'), may hold values from -6 to 6
- segments: int32 [4, 1024], P('dp'), may hold values from 0 to 4, as said below
- first_gain: bfloat16 [2048], replicated, may hold values from 0.5 to 1.5
- first_shift: bfloat16 [2048], replicated, may hold values from -3 to 3
- in_weight: bfloat16 [2048, 3, 2048], P(None, None, 'tensor'), may hold values from -0.125 to 0.125
- in_bias: bfloat16 [2, 2048], P(None, 'tensor'), may hold values from -2 to 2
- out_weight: bfloat16 [2048, 2048], P(None, 'tensor'), may hold values from -1 to 1
- out_bias: bfloat16 [2048], replicated, may hold values from -2 to 2
- second_gain: bfloat16 [2048], replicated, may hold values from 0.5 to 1.5
- second_shift: bfloat16 [2048], replicated, may hold values from -3 to 3
- up_weight: bfloat16 [2048, 8192], P(None, 'tensor'), may hold values from -0.125 to 0.125
- up_bias: bfloat16 [8192], P('tensor'), may hold values from -3 to 3
- down_weight: bfloat16 [2048, 8192], P(None, 'tensor'), may hold values from -0.0625 to 0.0625
- down_bias: bfloat16 [2048], replicated, may hold values from -2 to 2
- cotangent: bfloat16 [4, 1024, 2048], P('dp', 'ctx'), may hold values from -6 to 6
Outputs:
- outputs: bfloat16 [4, 1024, 2048], P('dp', ('ctx', 'tensor'))
- input_grad: bfloat16 [4, 1024, 2048], P('dp', ('ctx', 'tensor'))
- first_gain_grad: float32 [2048], replicated
- first_shift_grad: float32 [2048], replicated
- in_weight_grad: float32 [2048, 3, 2048], P(('dp', 'ctx'), None, 'tensor')
- in_bias_grad: float32 [2, 2048], P(None, 'tensor')
- out_weight_grad: float32 [2048, 2048], P(('dp', 'ctx'), 'tensor')
- out_bias_grad: float32 [2048], replicated
- second_gain_grad: float32 [2048], replicated
- second_shift_grad: float32 [2048], replicated
- up_weight_grad: float32 [2048, 8192], P(('dp', 'ctx'), 'tensor')
- up_bias_grad: float32 [8192], P('tensor')
- down_weight_grad: float32 [2048, 8192], P(('dp', 'ctx'), 'tensor')
- down_bias_grad: float32 [2048], replicated
Inputs may be any that keep to these rules, and one draw needn't show every extreme that they name: `segments`: along each sequence the numbers start at 0 and rise by one at each document boundary; every sequence holds exactly five documents.
All inputs are finite; a program needn't handle non-finite values.
Results may differ from a plain program's by a relative error of at most 0.019.
Values may be sent and summed in bfloat16 or wider, within the bound.
No kernel may reach another device: no remote copies, remote signals or barrier semaphores. Data moves between devices by JAX's collectives and lax.ppermute only.
A program may use at most 192 MiB of HBM per device.

v0:
```python
import math
import jax
import jax.numpy as jnp
from jax import lax
from jax.sharding import PartitionSpec as P

H = 16
HD = 128
EPSILON = 1e-05


def layer_norm(values, norm_gain, norm_shift):
    average = jnp.mean(values, axis=-1, keepdims=True)
    centered = values - average
    spread = jnp.mean(centered * centered, axis=-1, keepdims=True)
    return centered * lax.rsqrt(spread + EPSILON) * norm_gain + norm_shift


def contract(left, right, left_dim, right_dim):
    return lax.dot_general(
        left, right, (((left_dim,), (right_dim,)), ((), ())), preferred_element_type=jnp.float32
    )


def gelu_tanh(values):
    return jax.nn.gelu(values, approximate=True)


def shards(
    inputs,
    segments,
    first_gain,
    first_shift,
    in_weight,
    in_bias,
    out_weight,
    out_bias,
    second_gain,
    second_shift,
    up_weight,
    up_bias,
    down_weight,
    down_bias,
    cotangent,
):
    rows = inputs.shape[1]
    width = inputs.shape[2]
    local_width = in_weight.shape[2]
    local_hidden = up_weight.shape[1]
    heads_here = local_width // HD
    seq_length = segments.shape[1]
    share = rows // lax.axis_size("tensor")
    tensor_place = lax.axis_index("tensor")
    share_start = tensor_place * share
    scale = 1.0 / math.sqrt(HD)
    context_place = lax.axis_index("ctx")
    first_head = (tensor_place * heads_here).astype(jnp.float32)
    slopes = jnp.exp2(-8.0 * (first_head + jnp.arange(heads_here, dtype=jnp.float32) + 1.0) / H)
    segment_row = segments[0]
    query_pos = context_place * rows + jnp.arange(rows, dtype=jnp.int32)
    query_seg = lax.dynamic_slice_in_dim(segment_row, context_place * rows, rows)
    residual = inputs[0].astype(jnp.float32)
    residual_share = lax.dynamic_slice_in_dim(residual, share_start, share, 0)
    first_norm = (first_gain.astype(jnp.float32), first_shift.astype(jnp.float32))
    second_norm = (second_gain.astype(jnp.float32), second_shift.astype(jnp.float32))
    normed_first = layer_norm(residual, first_norm[0], first_norm[1]).astype(jnp.bfloat16)
    projected = jnp.einsum(
        "td,dcf->tcf", normed_first, in_weight, preferred_element_type=jnp.float32
    )
    bias_pair = in_bias.astype(jnp.float32)
    query_grid = (projected[:, 0] + bias_pair[0]).astype(jnp.bfloat16).reshape(rows, heads_here, HD)
    key_grid = projected[:, 1].astype(jnp.bfloat16).reshape(rows, heads_here, HD)
    value_grid = (projected[:, 2] + bias_pair[1]).astype(jnp.bfloat16).reshape(rows, heads_here, HD)
    keys_all, values_all = (
        lax.all_gather(key_grid, "ctx", axis=0, tiled=True),
        lax.all_gather(value_grid, "ctx", axis=0, tiled=True),
    )
    key_block = min(seq_length, max(rows, 512))
    needed = keys_all.shape[0] // key_block

    def block_scores(block):
        start = block * key_block
        key_part = lax.dynamic_slice_in_dim(keys_all, start, key_block, 0)
        value_part = lax.dynamic_slice_in_dim(values_all, start, key_block, 0)
        key_pos = start + jnp.arange(key_block, dtype=jnp.int32)
        key_seg = lax.dynamic_slice_in_dim(segment_row, start, key_block)
        raw = (
            jnp.einsum("qhd,khd->hqk", query_grid, key_part, preferred_element_type=jnp.float32)
            * scale
        )
        offset = (key_pos[None, :] - query_pos[:, None]).astype(jnp.float32)
        raw = raw + slopes[:, None, None] * offset[None]
        allowed = (
            (key_pos[None, :] <= query_pos[:, None]) & (key_seg[None, :] == query_seg[:, None])
        )[None]
        return (jnp.where(allowed, raw, -1e30), allowed, start, key_part, value_part)

    def stats_step(block, carry):
        top, total = carry
        scores, allowed, start, key_part, value_part = block_scores(block)
        new_top = jnp.maximum(top, jnp.max(scores, axis=-1))
        fresh = jnp.where(allowed, jnp.exp(scores - new_top[:, :, None]), 0.0)
        return (new_top, total * jnp.exp(top - new_top) + jnp.sum(fresh, axis=-1))

    start_top = jnp.full((heads_here, rows), -1e30, jnp.float32)
    start_total = jnp.zeros((heads_here, rows), jnp.float32)
    top, total = lax.fori_loop(0, needed, stats_step, (start_top, start_total))

    def probs_for(scores, allowed):
        return jnp.where(allowed, jnp.exp(scores - top[:, :, None]), 0.0) / total[:, :, None]

    def mix_step(block, carry):
        high_part, rest_part = carry
        scores, allowed, start, key_part, value_part = block_scores(block)
        probs = probs_for(scores, allowed)
        probs_low = lax.optimization_barrier(probs.astype(jnp.bfloat16))
        rest_low = (probs - probs_low.astype(jnp.float32)).astype(jnp.bfloat16)
        high_part = high_part + jnp.einsum(
            "hqk,khd->qhd", probs_low, value_part, preferred_element_type=jnp.float32
        )
        rest_part = rest_part + jnp.einsum(
            "hqk,khd->qhd", rest_low, value_part, preferred_element_type=jnp.float32
        )
        return (high_part, rest_part)

    empty_mix = jnp.zeros((rows, heads_here, HD), jnp.float32)
    mixed_high, mixed_rest = lax.fori_loop(0, needed, mix_step, (empty_mix, empty_mix))
    mixed_exact = (mixed_high + mixed_rest).reshape(rows, local_width)
    mixed_low = mixed_high.reshape(rows, local_width).astype(jnp.bfloat16)
    attention_share = lax.psum_scatter(
        contract(mixed_low, out_weight, 1, 1).astype(jnp.bfloat16),
        "tensor",
        scatter_dimension=0,
        tiled=True,
    ).astype(jnp.float32)
    middle_share = residual_share + attention_share + out_bias.astype(jnp.float32)
    normed_share, second_pull = jax.vjp(layer_norm, middle_share, second_norm[0], second_norm[1])
    normed_second = lax.all_gather(normed_share.astype(jnp.bfloat16), "tensor", axis=0, tiled=True)
    upper = jnp.dot(normed_second, up_weight, preferred_element_type=jnp.float32) + up_bias.astype(
        jnp.float32
    )
    active_full, gelu_pull = jax.vjp(gelu_tanh, upper)
    active = active_full.astype(jnp.bfloat16)
    feed_share = lax.psum_scatter(
        contract(active, down_weight, 1, 1).astype(jnp.bfloat16),
        "tensor",
        scatter_dimension=0,
        tiled=True,
    ).astype(jnp.float32)
    outputs = (middle_share + feed_share + down_bias.astype(jnp.float32)).astype(jnp.bfloat16)
    cotangent_low = cotangent[0]
    cotangent_share = lax.dynamic_slice_in_dim(cotangent_low, share_start, share, 0).astype(
        jnp.float32
    )
    down_whole = contract(cotangent_low, active, 0, 0)
    down_bias_term = jnp.sum(cotangent_share, axis=0)
    grad_active = jnp.dot(cotangent_low, down_weight, preferred_element_type=jnp.float32)
    grad_upper = gelu_pull(grad_active)[0].astype(jnp.bfloat16)
    up_bias_term = jnp.sum(grad_upper.astype(jnp.float32), axis=0)
    up_whole = contract(normed_second, grad_upper, 0, 0)
    grad_normed_share = lax.psum_scatter(
        contract(grad_upper, up_weight, 1, 1).astype(jnp.bfloat16),
        "tensor",
        scatter_dimension=0,
        tiled=True,
    ).astype(jnp.float32)
    grad_from_second, second_gain_term, second_shift_term = second_pull(grad_normed_share)
    grad_middle_share = cotangent_share + grad_from_second
    out_bias_term = jnp.sum(grad_middle_share, axis=0)
    grad_middle_low = lax.all_gather(
        grad_middle_share.astype(jnp.bfloat16), "tensor", axis=0, tiled=True
    )
    grad_mixed = jnp.dot(grad_middle_low, out_weight, preferred_element_type=jnp.float32).astype(
        jnp.bfloat16
    )
    out_whole = contract(grad_middle_low, mixed_low, 0, 0)
    delta = jnp.sum(
        (grad_mixed.astype(jnp.float32) * mixed_exact).reshape(rows, heads_here, HD), axis=-1
    ).T
    grad_mixed_grid = grad_mixed.reshape(rows, heads_here, HD)

    def back_step(block, carry):
        grad_query, grad_keys, grad_values = carry
        scores, allowed, start, key_part, value_part = block_scores(block)
        probs = probs_for(scores, allowed)
        probs_low = probs.astype(jnp.bfloat16)
        grad_probs = jnp.einsum(
            "qhd,khd->hqk", grad_mixed_grid, value_part, preferred_element_type=jnp.float32
        )
        grad_scores = (probs * (grad_probs - delta[:, :, None])).astype(jnp.bfloat16)
        grad_query = (
            grad_query
            + jnp.einsum("hqk,khd->qhd", grad_scores, key_part, preferred_element_type=jnp.float32)
            * scale
        )
        key_term = (
            jnp.einsum("hqk,qhd->khd", grad_scores, query_grid, preferred_element_type=jnp.float32)
            * scale
        )
        value_term = jnp.einsum(
            "hqk,qhd->khd", probs_low, grad_mixed_grid, preferred_element_type=jnp.float32
        )
        grad_keys = lax.dynamic_update_slice_in_dim(
            grad_keys, lax.dynamic_slice_in_dim(grad_keys, start, key_block, 0) + key_term, start, 0
        )
        grad_values = lax.dynamic_update_slice_in_dim(
            grad_values,
            lax.dynamic_slice_in_dim(grad_values, start, key_block, 0) + value_term,
            start,
            0,
        )
        return (grad_query, grad_keys, grad_values)

    empty_keys = jnp.zeros((keys_all.shape[0], heads_here, HD), jnp.float32)
    grad_query, grad_keys, grad_values = lax.fori_loop(
        0, needed, back_step, (empty_mix, empty_keys, empty_keys)
    )
    key_grad_part, value_grad_part = (
        lax.psum_scatter(
            grad_keys.astype(jnp.bfloat16), "ctx", scatter_dimension=0, tiled=True
        ).astype(jnp.float32),
        lax.psum_scatter(
            grad_values.astype(jnp.bfloat16), "ctx", scatter_dimension=0, tiled=True
        ).astype(jnp.float32),
    )
    grad_projected = jnp.stack(
        [
            grad_query.reshape(rows, local_width),
            key_grad_part.reshape(rows, local_width),
            value_grad_part.reshape(rows, local_width),
        ],
        axis=1,
    ).astype(jnp.bfloat16)
    in_bias_term = jnp.sum(grad_projected[:, 0::2].astype(jnp.float32), axis=0)
    in_whole = jnp.einsum(
        "td,tcf->dcf", normed_first, grad_projected, preferred_element_type=jnp.float32
    )
    grad_first_share = lax.psum_scatter(
        jnp.einsum(
            "tcf,dcf->td", grad_projected, in_weight, preferred_element_type=jnp.float32
        ).astype(jnp.bfloat16),
        "tensor",
        scatter_dimension=0,
        tiled=True,
    ).astype(jnp.float32)
    normed_again, first_pull = jax.vjp(layer_norm, residual_share, first_norm[0], first_norm[1])
    grad_from_first, first_gain_term, first_shift_term = first_pull(grad_first_share)
    input_grad = (grad_middle_share + grad_from_first).astype(jnp.bfloat16)
    in_weight_grad, out_weight_grad, up_weight_grad, down_weight_grad = (
        lax.psum_scatter(
            in_whole.astype(jnp.bfloat16), ("dp", "ctx"), scatter_dimension=0, tiled=True
        ).astype(jnp.float32),
        lax.psum_scatter(
            out_whole.astype(jnp.bfloat16), ("dp", "ctx"), scatter_dimension=0, tiled=True
        ).astype(jnp.float32),
        lax.psum_scatter(
            up_whole.astype(jnp.bfloat16), ("dp", "ctx"), scatter_dimension=0, tiled=True
        ).astype(jnp.float32),
        lax.psum_scatter(
            down_whole.astype(jnp.bfloat16), ("dp", "ctx"), scatter_dimension=0, tiled=True
        ).astype(jnp.float32),
    )
    in_bias_whole = lax.dynamic_update_slice(
        jnp.zeros((2, width), jnp.float32), in_bias_term, (0, tensor_place * local_width)
    )
    up_bias_whole = lax.dynamic_update_slice(
        jnp.zeros((local_hidden * lax.axis_size("tensor"),), jnp.float32),
        up_bias_term,
        (tensor_place * local_hidden,),
    )
    small_sums = lax.psum(
        (
            first_gain_term,
            first_shift_term,
            in_bias_whole,
            out_bias_term,
            second_gain_term,
            second_shift_term,
            up_bias_whole,
            down_bias_term,
        ),
        ("dp", "ctx", "tensor"),
    )
    in_bias_grad = lax.dynamic_slice_in_dim(
        small_sums[2], tensor_place * local_width, local_width, 1
    )
    up_bias_grad = lax.dynamic_slice_in_dim(
        small_sums[6], tensor_place * local_hidden, local_hidden, 0
    )
    return (
        outputs[None],
        input_grad[None],
        small_sums[0],
        small_sums[1],
        in_weight_grad,
        in_bias_grad,
        out_weight_grad,
        small_sums[3],
        small_sums[4],
        small_sums[5],
        up_weight_grad,
        up_bias_grad,
        down_weight_grad,
        small_sums[7],
    )


def solution(mesh):
    return jax.shard_map(
        shards,
        mesh=mesh,
        in_specs=(
            P("dp", "ctx", None),
            P("dp", None),
            P(),
            P(),
            P(None, None, "tensor"),
            P(None, "tensor"),
            P(None, "tensor"),
            P(),
            P(),
            P(),
            P(None, "tensor"),
            P("tensor"),
            P(None, "tensor"),
            P(),
            P("dp", "ctx", None),
        ),
        out_specs=(
            P("dp", ("ctx", "tensor"), None),
            P("dp", ("ctx", "tensor"), None),
            P(),
            P(),
            P(("dp", "ctx"), None, "tensor"),
            P(None, "tensor"),
            P(("dp", "ctx"), "tensor"),
            P(),
            P(),
            P(),
            P(("dp", "ctx"), "tensor"),
            P("tensor"),
            P(("dp", "ctx"), "tensor"),
            P(),
        ),
        check_vma=False,
    )
```

profile of v0, /device:TPU:0, one launch (start us, length us, event | category | flops | bytes accessed | tf_op | source)
XLA Modules:
  0.0 1117.3 jit_solution(4887311695506873772)
XLA Ops:
  11.7 7.0 fusion.87
  25.9 21.1 %all-gather.7.cloned.1.call-done = bf16[1024,8,128]{2,0,1:T(8,128)(2,1)} async-done(((bf16[256,8,128]{2,0,1:T(8,128)(2,1)}), bf16[1024,8,128]{2,0,1:T(8,128)(2,1)}) %all-gather.7.cloned.1.call-update) | async-done | bytes 2097168 | tf_op jit(solution)/shard_map/all_gather | solution.py:75
  47.0 16.6 %while.50 = (s32[]{:T(128)}, f32[8,256]{1,0:T(8,128)S(1)}, f32[8,256]{1,0:T(8,128)S(1)}, s32[1024]{0:T(1024)S(1)}, s32[256]{0:T(256)S(1)}, /*index=5*/bf16[1024,...) while((s32[]{:T(128)}, f32[8,256]{1,0:T(8,128)S(1)}, ...), condition=%wide.region_5.6_spmd.clone, body=%wide.region_2.5_spmd.clone.sunk | while | flops 281684768 | bytes 12050738 | solution.py:107
  47.4 4.3 fusion.148
  51.7 3.5 select_reduce_fusion.2
  55.7 4.3 fusion.148
  60.1 3.5 select_reduce_fusion.2
  63.6 8.1 all-gather.5.cloned.1.call-done
  71.7 25.1 %while.51 = (s32[]{:T(128)}, f32[256,8,128]{0,2,1:T(8,128)}, f32[256,8,128]{0,2,1:T(8,128)S(1)}, bf16[1024,8,128]{2,0,1:T(8,128)(2,1)}, s32[1024]{0:T(1024)S(1)}...) while((s32[]{:T(128)}, f32[256,8,128]{0,2,1:T(8,128)}, ...), condition=%wide.region_7.8_spmd.clone, body=%wide.region_6.7_spmd.clone.sunk | while | flops 818545408 | bytes 32276812 | solution.py:127
  73.0 5.1 fusion.154
  80.9 3.2 fusion.156
  85.4 5.1 fusion.154
  90.4 3.2 fusion.155
  93.6 3.2 fusion.156
  99.5 4.7 convolution_convert_fusion.5
  104.8 19.9 %reduce-scatter.13.cloned.1.call-done = bf16[128,2048]{1,0:T(8,128)(2,1)} async-done(((bf16[256,2048]{1,0:T(8,128)(2,1)}), bf16[128,2048]{1,0:T(8,128)(2,1)}) %reduce-scatter.13.cloned.1.call-update) | async-done | bytes 524304 | tf_op jit(solution)/shard_map/reduce_scatter | solution.py:130
  127.4 21.4 %all-gather.9.cloned.1.call-done = bf16[256,2048]{1,0:T(8,128)(2,1)} async-done(((bf16[128,2048]{1,0:T(8,128)(2,1)}), bf16[256,2048]{1,0:T(8,128)(2,1)}) %all-gather.9.cloned.1.call-update) | async-done | bytes 1048592 | tf_op jit(solution)/shard_map/all_gather | solution.py:138
  148.8 8.5 convolution_add_fusion
  157.3 12.7 %convert_reduce_fusion = (f32[4096]{0:T(1024)S(1)}, bf16[256,4096]{1,0:T(8,128)(2,1)}) fusion(f32[256,4096]{1,0:T(8,128)S(1)} %convolution_add_fusion, bf16[2048,4096]{1,0:T(8,128)(2,1)} %param.33, bf16[1,256,2048]{2,1,0:T(8,128)(2,1)S(1)} %copy-done.22), kind=kOutput, calls=%fused_computation.85 | convolution fusion | flops 4318031872 | bytes 24133632 | tf_op jit(solution)/shard_map/dot_general | solution.py:157
  170.0 11.9 %convolution_convert_fusion.3 = bf16[256,2048]{1,0:T(8,128)(2,1)} fusion(bf16[256,4096]{1,0:T(8,128)(2,1)} %get-tuple-element.946, bf16[2048,4096]{1,0:T(8,128)(2,1)} %param.31), kind=kOutput, calls=%fused_computation.89 | convolution fusion | flops 4295491584 | bytes 19922944 | tf_op jit(solution)/shard_map/dot_general | solution.py:20
  182.2 13.3 %convolution_convert_fusion.4 = bf16[256,2048]{1,0:T(8,128)(2,1)} fusion(bf16[2048,4096]{1,0:T(8,128)(2,1)} %param.33, f32[256,4096]{1,0:T(8,128)} %copy-done.47), kind=kOutput, calls=%fused_computation.90 | convolution fusion | flops 4304928768 | bytes 22020096 | tf_op jit(solution)/shard_map/dot_general | solution.py:20
  195.7 6.8 reduce-scatter.17.cloned.1.call-done
  206.7 18.2 %reduce-scatter.15.cloned.1.call-done = bf16[128,2048]{1,0:T(8,128)(2,1)} async-done(((bf16[256,2048]{1,0:T(8,128)(2,1)}), bf16[128,2048]{1,0:T(8,128)(2,1)}) %reduce-scatter.15.cloned.1.call-update) | async-done | bytes 524304 | tf_op jit(solution)/shard_map/reduce_scatter | solution.py:144
  224.9 3.2 fusion.89
  230.6 20.8 %all-gather.11.cloned.1.call-done = bf16[256,2048]{1,0:T(8,128)(2,1)} async-done(((bf16[128,2048]{1,0:T(8,128)(2,1)}), bf16[256,2048]{1,0:T(8,128)(2,1)}) %all-gather.11.cloned.1.call-update) | async-done | bytes 1048592 | tf_op jit(solution)/shard_map/all_gather | solution.py:170
  251.4 3.8 convolution_convert_fusion.6
  260.6 32.2 %while.52 = (s32[]{:T(128)}, f32[256,8,128]{0,2,1:T(8,128)}, f32[1024,8,128]{2,0,1:T(8,128)}, f32[1024,8,128]{2,0,1:T(8,128)}, bf16[1024,8,128]{2,0,1:T(8,128)(2...) while((s32[]{:T(128)}, f32[256,8,128]{0,2,1:T(8,128)}, ...), condition=%wide.region_17.18_spmd.clone, body=%wide.region_16.17_spmd.clone.sunk | while | flops 1356727040 | bytes 111452632 | solution.py:215
  261.1 3.0 fusion.167
  269.8 3.9 fusion.170
  277.1 3.0 fusion.167
  282.8 3.2 fusion.169
  286.1 3.9 fusion.170
  292.9 3.8 convert_element_type.252
  296.8 4.0 convert_element_type.251
  301.6 26.7 %reduce-scatter.21.cloned.1.call-done = bf16[256,8,128]{2,0,1:T(8,128)(2,1)} async-done(((bf16[1024,8,128]{2,0,1:T(8,128)(2,1)}), bf16[256,8,128]{2,0,1:T(8,128)(2,1)}) %reduce-scatter.21.cloned.1.call-update) | async-done | bytes 524304 | tf_op jit(solution)/shard_map/reduce_scatter | solution.py:222
  329.9 32.4 %reduce-scatter.19.cloned.1.call-done = bf16[256,8,128]{2,0,1:T(8,128)(2,1)} async-done(((bf16[1024,8,128]{2,0,1:T(8,128)(2,1)}), bf16[256,8,128]{2,0,1:T(8,128)(2,1)}) %reduce-scatter.19.cloned.1.call-update) | async-done | bytes 524304 | tf_op jit(solution)/shard_map/reduce_scatter | solution.py:219
  364.0 9.2 fusion.60
  373.3 3.2 convolution_convert_fusion.2
  381.9 11.7 %reduce-scatter.23.cloned.1.call-done = bf16[128,2048]{1,0:T(8,128)(2,1)} async-done(((bf16[256,2048]{1,0:T(8,128)(2,1)}), bf16[128,2048]{1,0:T(8,128)(2,1)}) %reduce-scatter.23.cloned.1.call-update) | async-done | bytes 524304 | tf_op jit(solution)/shard_map/reduce_scatter | solution.py:238
  398.1 14.2 %convert_bitcast_fusion = bf16[2048,4096]{0,1:T(8,128)(2,1)} fusion(bf16[1,256,2048]{2,1,0:T(8,128)(2,1)} %param.35, f32[256,4096]{1,0:T(8,128)} %copy-done.47), kind=kOutput, calls=%fused_computation.72 | convolution fusion | flops 4312793088 | bytes 22020096 | tf_op jit(solution)/shard_map/dot_general | solution.py:20
  412.3 21.6 %copy.68 = bf16[2048,4096]{1,0:T(8,128)(2,1)} copy(bf16[2048,4096]{0,1:T(8,128)(2,1)} %convert_bitcast_fusion) | data formatting | bytes 33554432
  435.2 9.9 convolution_convert_fusion
  446.3 7.9 convolution_convert_fusion.1
  454.3 15.7 %reduce-scatter.27.cloned.1.call-done = bf16[128,1024]{1,0:T(8,128)(2,1)} async-done(((bf16[2048,1024]{1,0:T(8,128)(2,1)}), bf16[128,1024]{1,0:T(8,128)(2,1)}) %reduce-scatter.27.cloned.1.call-update) | async-done | bytes 262160 | tf_op jit(solution)/shard_map/reduce_scatter | solution.py:253
  474.1 127.4 %all-reduce.3.cloned.1.call-done = (f32[2048]{0:T(1024)}, f32[2048]{0:T(1024)}, f32[2,2048]{1,0:T(2,128)}, f32[2048]{0:T(1024)}, f32[2048]{0:T(1024)}, /*index=5*/f32[2048]{0:T(1024)}, f32[8192]{0:T(1024)}, f32[2048]{0:T(1024)}) async-done(((f32[2048]{0:T(1024)}, f32[2048]{0:T(1024)}, f32[2,2048]{1,0:T(2,128)}, f32[2048]{0:T(1024)}, f32[2048]{0:T(1024)}, /*index=5*/f32[2048]{0:T(1024)}, f32[8192]{0:T(1024)}, ...) | async-done | bytes 98320 | tf_op jit(solution)/shard_map/psum | solution.py:271
  604.1 181.2 %reduce-scatter.31.cloned.1.call-done = bf16[128,4096]{1,0:T(8,128)(2,1)} async-done(((bf16[2048,4096]{1,0:T(8,128)(2,1)}), bf16[128,4096]{1,0:T(8,128)(2,1)}) %reduce-scatter.31.cloned.1.call-update) | async-done | bytes 1048592
  788.5 178.3 %reduce-scatter.29.cloned.1.call-done = bf16[128,4096]{1,0:T(8,128)(2,1)} async-done(((bf16[2048,4096]{1,0:T(8,128)(2,1)}), bf16[128,4096]{1,0:T(8,128)(2,1)}) %reduce-scatter.29.cloned.1.call-update) | async-done | bytes 1048592 | tf_op jit(solution)/shard_map/reduce_scatter | solution.py:256
  969.6 134.9 %reduce-scatter.25.cloned.1.call-done = bf16[128,3,1024]{2,0,1:T(8,128)(2,1)} async-done(((bf16[2048,3,1024]{2,0,1:T(8,128)(2,1)}), bf16[128,3,1024]{2,0,1:T(8,128)(2,1)}) %reduce-scatter.25.cloned.1.call-update) | async-done | bytes 786448 | tf_op jit(solution)/shard_map/reduce_scatter | solution.py:250
  (265 shorter events, 86.1 us)
Async XLA Ops:
  7.2 39.8 %all-gather.7.cloned.1.call-start = ((), (), s32[]{:S(2)}) async-start(), calls=%async_computation.11 | async-start | bytes 2621440 | tf_op jit(solution)/shard_map/all_gather | solution.py:75
  7.9 10.8 copy-start.31
  8.6 10.1 copy-start.25
  10.1 8.7 copy-start.43
  11.7 7.0 copy-start.45
  21.5 50.2 %all-gather.5.cloned.1.call-start = ((), (), s32[]{:S(2)}) async-start(), calls=%async_computation.10 | async-start | bytes 2621440 | tf_op jit(solution)/shard_map/all_gather | solution.py:76
  24.5 100.2 %reduce-scatter.13.cloned.1.call-start = ((), (), s32[]{:S(2)}) async-start(), calls=%async_computation.12 | async-start | bytes 1572864 | tf_op jit(solution)/shard_map/reduce_scatter | solution.py:130
  99.5 5.2 copy-start.39
  99.5 5.2 copy-start.40
  99.5 5.3 copy-start.41
  104.2 23.1 %copy-start.30 = (bf16[4096]{0:T(1024)(128)(2,1)S(1)}, bf16[4096]{0:T(1024)(128)(2,1)}, u32[]{:S(2)}) copy-start(bf16[4096]{0:T(1024)(128)(2,1)} %param.32) | copy-start | bytes 24580
  104.2 44.5 %all-gather.9.cloned.1.call-start = ((), (), s32[]{:S(2)}) async-start(), calls=%async_computation.13 | async-start | bytes 1572864 | tf_op jit(solution)/shard_map/all_gather | solution.py:138
  104.7 52.6 %copy-start.7 = (f32[1,256,2048]{2,1,0:T(8,128)}, f32[1,256,2048]{2,1,0:T(8,128)S(1)}, u32[]{:S(2)}) copy-start(f32[1,256,2048]{2,1,0:T(8,128)S(1)} %convert_element_type.219) | copy-start | bytes 6291460
  127.3 75.1 %reduce-scatter.17.cloned.1.call-start = ((), (), s32[]{:S(2)}) async-start(), calls=%async_computation.15 | async-start | bytes 1572864 | tf_op jit(solution)/shard_map/reduce_scatter | solution.py:161
  148.8 8.5 copy-start.22
  157.3 12.7 %copy-start.47 = (f32[256,4096]{1,0:T(8,128)}, f32[256,4096]{1,0:T(8,128)S(1)}, u32[]{:S(2)}) copy-start(f32[256,4096]{1,0:T(8,128)S(1)} %convolution_add_fusion) | copy-start | bytes 12582916
  182.0 13.7 %copy-start.42 = (bf16[2048]{0:T(1024)(128)(2,1)S(1)}, bf16[2048]{0:T(1024)(128)(2,1)}, u32[]{:S(2)}) copy-start(bf16[2048]{0:T(1024)(128)(2,1)} %param.34) | copy-start | bytes 12292
  182.0 42.9 %reduce-scatter.15.cloned.1.call-start = ((), (), s32[]{:S(2)}) async-start(), calls=%async_computation.14 | async-start | bytes 1572864 | tf_op jit(solution)/shard_map/reduce_scatter | solution.py:144
  195.6 29.3 %copy-start.23 = (bf16[1,256,2048]{2,1,0:T(8,128)(2,1)S(1)}, bf16[1,256,2048]{2,1,0:T(8,128)(2,1)}, u32[]{:S(2)}) copy-start(bf16[1,256,2048]{2,1,0:T(8,128)(2,1)} %param.35) | copy-start | bytes 3145732
  195.6 55.8 %all-gather.11.cloned.1.call-start = ((), (), s32[]{:S(2)}) async-start(), calls=%async_computation.16 | async-start | bytes 1572864 | tf_op jit(solution)/shard_map/all_gather | solution.py:170
  204.4 25.8 %copy-start.13 = (f32[256,8,128]{0,2,1:T(8,128)S(1)}, f32[256,8,128]{0,2,1:T(8,128)}, u32[]{:S(2)}) copy-start(f32[256,8,128]{0,2,1:T(8,128)} %get-tuple-element.938) | copy-start | bytes 3145732
  229.9 98.4 %reduce-scatter.21.cloned.1.call-start = ((), (), s32[]{:S(2)}) async-start(), calls=%async_computation.18 | async-start | bytes 2621440 | tf_op jit(solution)/shard_map/reduce_scatter | solution.py:222
  261.1 5.0 copy-start.3
  266.8 6.9 copy-start.4
  277.1 5.0 copy-start.3
  282.8 7.2 copy-start.4
  296.7 65.6 %reduce-scatter.19.cloned.1.call-start = ((), (), s32[]{:S(2)}) async-start(), calls=%async_computation.17 | async-start | bytes 2621440 | tf_op jit(solution)/shard_map/reduce_scatter | solution.py:219
  300.8 92.9 %reduce-scatter.23.cloned.1.call-start = ((), (), s32[]{:S(2)}) async-start(), calls=%async_computation.19 | async-start | bytes 1572864 | tf_op jit(solution)/shard_map/reduce_scatter | solution.py:238
  301.6 78.8 %copy-start.18 = (bf16[256,1,1024]{2,0,1:T(8,128)(2,1)}, bf16[256,1,1024]{2,0,1:T(8,128)(2,1)S(1)}, u32[]{:S(2)}) copy-start(bf16[256,1,1024]{2,0,1:T(8,128)(2,1)S(1)} %copy.66) | copy-start | bytes 1572868
  329.9 50.5 %copy-start.19 = (bf16[256,1,1024]{2,0,1:T(8,128)(2,1)}, bf16[256,1,1024]{2,0,1:T(8,128)(2,1)S(1)}, u32[]{:S(2)}) copy-start(bf16[256,1,1024]{2,0,1:T(8,128)(2,1)S(1)} %stack_reshape.14) | copy-start | bytes 1572868
  364.0 9.2 copy-start.20
  364.0 9.3 copy-start.14
  364.0 9.3 copy-start.17
  373.2 96.8 %reduce-scatter.27.cloned.1.call-start = ((), (), s32[]{:S(2)}) async-start(), calls=%async_computation.21 | async-start | bytes 4456448 | tf_op jit(solution)/shard_map/reduce_scatter | solution.py:253
  376.5 17.1 %copy-start.26 = (f32[2048]{0:T(1024)S(1)}, f32[2048]{0:T(1024)}, u32[]{:S(2)}) copy-start(f32[2048]{0:T(1024)} %copy-done.25) | copy-start | bytes 24580
  376.6 224.9 %all-reduce.3.cloned.1.call-start = ((), (), s32[]{:S(2)}) async-start(), calls=%async_computation.24 | async-start | bytes 196608 | tf_op jit(solution)/shard_map/psum | solution.py:271
  380.4 17.5 %copy-start.27 = (f32[8192]{0:T(1024)}, f32[8192]{0:T(1024)S(1)}, u32[]{:S(2)}) copy-start(f32[8192]{0:T(1024)S(1)} %dynamic_update_slice.21) | copy-start | bytes 98308
  381.9 16.0 %copy-start.28 = (f32[2,2048]{1,0:T(2,128)}, f32[2,2048]{1,0:T(2,128)S(1)}, u32[]{:S(2)}) copy-start(f32[2,2048]{1,0:T(2,128)S(1)} %constant_dynamic-update-slice_fusion) | copy-start | bytes 49156
  397.9 387.3 %reduce-scatter.31.cloned.1.call-start = ((), (), s32[]{:S(2)}) async-start(), calls=%async_computation.23 | async-start | bytes 17825792
  434.0 532.8 %reduce-scatter.29.cloned.1.call-start = ((), (), s32[]{:S(2)}) async-start(), calls=%async_computation.22 | async-start | bytes 17825792 | tf_op jit(solution)/shard_map/reduce_scatter | solution.py:256
  445.1 659.4 %reduce-scatter.25.cloned.1.call-start = ((), (), s32[]{:S(2)}) async-start(), calls=%async_computation.20 | async-start | bytes 13369344 | tf_op jit(solution)/shard_map/reduce_scatter | solution.py:250
  454.3 17.6 %copy-start.12 = (f32[128,2048]{1,0:T(8,128)S(1)}, f32[128,2048]{1,0:T(8,128)}, u32[]{:S(2)}) copy-start(f32[128,2048]{1,0:T(8,128)} %copy-done.11) | copy-start | bytes 3145732
  786.8 320.1 %copy-start.38 = (f32[2048]{0:T(1024)S(1)}, f32[2048]{0:T(1024)}, u32[]{:S(2)}) copy-start(f32[2048]{0:T(1024)} %get-tuple-element.1320) | copy-start | bytes 24580
  786.9 320.7 %copy-start.37 = (f32[2048]{0:T(1024)S(1)}, f32[2048]{0:T(1024)}, u32[]{:S(2)}) copy-start(f32[2048]{0:T(1024)} %get-tuple-element.1321) | copy-start | bytes 24580
  786.9 321.3 %copy-start.36 = (f32[2048]{0:T(1024)S(1)}, f32[2048]{0:T(1024)}, u32[]{:S(2)}) copy-start(f32[2048]{0:T(1024)} %get-tuple-element.1325) | copy-start | bytes 24580
  786.9 321.9 %copy-start.35 = (f32[2048]{0:T(1024)S(1)}, f32[2048]{0:T(1024)}, u32[]{:S(2)}) copy-start(f32[2048]{0:T(1024)} %get-tuple-element.1326) | copy-start | bytes 24580
  786.9 322.5 %copy-start.34 = (f32[2048]{0:T(1024)S(1)}, f32[2048]{0:T(1024)}, u32[]{:S(2)}) copy-start(f32[2048]{0:T(1024)} %get-tuple-element.1327) | copy-start | bytes 24580
  786.9 323.1 %copy-start.33 = (f32[2048]{0:T(1024)S(1)}, f32[2048]{0:T(1024)}, u32[]{:S(2)}) copy-start(f32[2048]{0:T(1024)} %get-tuple-element.1331) | copy-start | bytes 24580
  (21 other events, 50.8 us)
Sparse Core Ops, SparseCore 0:
  21.6 25.2 all-gather.6
  49.1 22.5 all-gather.4
  104.3 20.3 reduce-scatter.12
  127.4 21.2 all-gather.8
  182.1 20.3 reduce-scatter.16
  204.5 20.3 reduce-scatter.14
  230.1 21.2 all-gather.10
  296.9 31.4 reduce-scatter.20
  330.9 31.4 reduce-scatter.18
  373.3 20.2 reduce-scatter.22
  397.5 72.4 reduce-scatter.26
  478.6 122.7 all-reduce.2
  605.5 179.6 reduce-scatter.30
  789.2 177.5 reduce-scatter.28
  970.7 133.7 reduce-scatter.24
where the time goes:
time: 1130 us; the launch traced here: 1120 us
  waiting for transfers between devices  825 us (73%)
  matrix products  161 us (14%)
  local copies, waits for them, and re-layouts  58.1 us (5%)
  other arithmetic  56.4 us (5%)
  between operations  14.9 us (1%)
    unnamed x16, waiting for transfers between devices  181 us
    reduce_scatter x1, waiting for transfers between devices, shards(): lax.psum_scatter(up_whole.astype(jnp.bfloat16), ('dp', 'ctx'), scatter_di...  178 us
    reduce_scatter x1, waiting for transfers between devices, shards(): lax.psum_scatter(in_whole.astype(jnp.bfloat16), ('dp', 'ctx'), scatter_di...  135 us
    psum x1, waiting for transfers between devices, shards(): lax.psum((first_gain_term, first_shift_term, in_bias_whole, out_bias_term...  127 us
    dot_general x6, matrix products, contract(): lax.dot_general(left, right, (((left_dim,), (right_dim,)), ((), ())), pre...  57.2 us
    unnamed x101, local copies, waits for them, and re-layouts  37.6 us
    reduce_scatter x1, waiting for transfers between devices, shards(): lax.psum_scatter(grad_keys.astype(jnp.bfloat16), 'ctx', scatter_dimension...  32.4 us
    reduce_scatter x1, waiting for transfers between devices, shards(): lax.psum_scatter(grad_values.astype(jnp.bfloat16), 'ctx', scatter_dimensi...  26.7 us
  transfers between devices with their start and end apart: 15, of which 15 were waited for; matrix products, arithmetic and copies ran while one was open for 11% of the time, Pallas kernels for 0%

commit v1 on v0

--- a/solution.py
+++ b/solution.py
@@ -268,19 +268,18 @@
         up_bias_term,
         (tensor_place * local_hidden,),
     )
-    small_sums = lax.psum(
-        (
-            first_gain_term,
-            first_shift_term,
-            in_bias_whole,
-            out_bias_term,
-            second_gain_term,
-            second_shift_term,
-            up_bias_whole,
-            down_bias_term,
-        ),
-        ("dp", "ctx", "tensor"),
-    )
+    small_sums = (
+        first_gain_term,
+        first_shift_term,
+        in_bias_whole,
+        out_bias_term,
+        second_gain_term,
+        second_shift_term,
+        up_bias_whole,
+        down_bias_term,
+    )
+    for q in (("ctx", "tensor"), "dp"):
+        small_sums = lax.psum(small_sums, axis_name=q)
     in_bias_grad = lax.dynamic_slice_in_dim(
         small_sums[2], tensor_place * local_width, local_width, 1
     )

time: 1130 us -> 1090 us (0.965)
  waiting for transfers between devices: 825 us -> 792 us
    psum x1 -> x2, waiting for transfers between devices: 127 us -> 82.6 us  [shards(): small_sums = lax.psum(small_sums, axis_name=q)]
    unnamed x101 -> x99, local copies, waits for them, and re-layouts: 37.6 us -> 36.2 us
    unnamed x16 -> x17, waiting for transfers between devices: 181 us -> 181 us
  transfers between devices with their start and end apart: 15 -> 16, of which waited for: 15 -> 16; matrix products, arithmetic and copies ran while one was open for 11% -> 11% of each run, Pallas kernels for 0% -> 0%
where the time goes in v1:
time: 1090 us; the launch traced here: 1080 us
  waiting for transfers between devices  792 us (73%)
  matrix products  159 us (15%)
  local copies, waits for them, and re-layouts  57.5 us (5%)
  other arithmetic  56.8 us (5%)
  between operations  14.8 us (1%)
    unnamed x17, waiting for transfers between devices  181 us
    reduce_scatter x1, waiting for transfers between devices, shards(): lax.psum_scatter(up_whole.astype(jnp.bfloat16), ('dp', 'ctx'), scatter_di...  179 us
    reduce_scatter x1, waiting for transfers between devices, shards(): lax.psum_scatter(in_whole.astype(jnp.bfloat16), ('dp', 'ctx'), scatter_di...  135 us
    psum x2, waiting for transfers between devices, shards(): small_sums = lax.psum(small_sums, axis_name=q)  82.6 us
    dot_general x6, matrix products, contract(): lax.dot_general(left, right, (((left_dim,), (right_dim,)), ((), ())), pre...  55.5 us
    unnamed x99, local copies, waits for them, and re-layouts  36.2 us
    reduce_scatter x1, waiting for transfers between devices, shards(): lax.psum_scatter(grad_keys.astype(jnp.bfloat16), 'ctx', scatter_dimension...  32.4 us
    reduce_scatter x1, waiting for transfers between devices, shards(): lax.psum_scatter(grad_values.astype(jnp.bfloat16), 'ctx', scatter_dimensi...  26.7 us
  transfers between devices with their start and end apart: 16, of which 16 were waited for; matrix products, arithmetic and copies ran while one was open for 11% of the time, Pallas kernels for 0%

profile of v1, /device:TPU:0, one launch (start us, length us, event | category | flops | bytes accessed | tf_op | source)
XLA Modules:
  0.0 1083.2 jit_solution(11420607034312700475)
XLA Ops:
  11.7 7.0 fusion.87
  25.9 21.1 %all-gather.7.cloned.1.call-done = bf16[1024,8,128]{2,0,1:T(8,128)(2,1)} async-done(((bf16[256,8,128]{2,0,1:T(8,128)(2,1)}), bf16[1024,8,128]{2,0,1:T(8,128)(2,1)}) %all-gather.7.cloned.1.call-update) | async-done | bytes 2097168 | tf_op jit(solution)/shard_map/all_gather | solution.py:75
  47.0 16.7 %while.50 = (s32[]{:T(128)}, f32[8,256]{1,0:T(8,128)S(1)}, f32[8,256]{1,0:T(8,128)S(1)}, s32[1024]{0:T(1024)S(1)}, s32[256]{0:T(256)S(1)}, /*index=5*/bf16[1024,...) while((s32[]{:T(128)}, f32[8,256]{1,0:T(8,128)S(1)}, ...), condition=%wide.region_5.6_spmd.clone, body=%wide.region_2.5_spmd.clone.sunk | while | flops 281684768 | bytes 12050738 | solution.py:107
  47.5 4.3 fusion.148
  51.7 3.5 select_reduce_fusion.2
  55.8 4.3 fusion.148
  60.1 3.5 select_reduce_fusion.2
  63.7 8.1 all-gather.5.cloned.1.call-done
  71.7 25.1 %while.51 = (s32[]{:T(128)}, f32[256,8,128]{0,2,1:T(8,128)}, f32[256,8,128]{0,2,1:T(8,128)S(1)}, bf16[1024,8,128]{2,0,1:T(8,128)(2,1)}, s32[1024]{0:T(1024)S(1)}...) while((s32[]{:T(128)}, f32[256,8,128]{0,2,1:T(8,128)}, ...), condition=%wide.region_7.8_spmd.clone, body=%wide.region_6.7_spmd.clone.sunk | while | flops 818545408 | bytes 32276812 | solution.py:127
  73.0 5.1 fusion.154
  80.9 3.2 fusion.156
  85.4 5.1 fusion.154
  90.5 3.2 fusion.155
  93.7 3.2 fusion.156
  99.6 4.7 convolution_convert_fusion.5
  104.8 19.9 %reduce-scatter.13.cloned.1.call-done = bf16[128,2048]{1,0:T(8,128)(2,1)} async-done(((bf16[256,2048]{1,0:T(8,128)(2,1)}), bf16[128,2048]{1,0:T(8,128)(2,1)}) %reduce-scatter.13.cloned.1.call-update) | async-done | bytes 524304 | tf_op jit(solution)/shard_map/reduce_scatter | solution.py:130
  127.4 21.4 %all-gather.9.cloned.1.call-done = bf16[256,2048]{1,0:T(8,128)(2,1)} async-done(((bf16[128,2048]{1,0:T(8,128)(2,1)}), bf16[256,2048]{1,0:T(8,128)(2,1)}) %all-gather.9.cloned.1.call-update) | async-done | bytes 1048592 | tf_op jit(solution)/shard_map/all_gather | solution.py:138
  148.8 8.5 convolution_add_fusion
  157.3 12.7 %convert_reduce_fusion = (f32[4096]{0:T(1024)S(1)}, bf16[256,4096]{1,0:T(8,128)(2,1)}) fusion(f32[256,4096]{1,0:T(8,128)S(1)} %convolution_add_fusion, bf16[2048,4096]{1,0:T(8,128)(2,1)} %param.33, bf16[1,256,2048]{2,1,0:T(8,128)(2,1)S(1)} %copy-done.20), kind=kOutput, calls=%fused_computation.85 | convolution fusion | flops 4318031872 | bytes 24133632 | tf_op jit(solution)/shard_map/dot_general | solution.py:157
  170.0 11.9 %convolution_convert_fusion.3 = bf16[256,2048]{1,0:T(8,128)(2,1)} fusion(bf16[256,4096]{1,0:T(8,128)(2,1)} %get-tuple-element.954, bf16[2048,4096]{1,0:T(8,128)(2,1)} %param.31), kind=kOutput, calls=%fused_computation.89 | convolution fusion | flops 4295491584 | bytes 19922944 | tf_op jit(solution)/shard_map/dot_general | solution.py:20
  182.2 13.3 %convolution_convert_fusion.4 = bf16[256,2048]{1,0:T(8,128)(2,1)} fusion(bf16[2048,4096]{1,0:T(8,128)(2,1)} %param.33, f32[256,4096]{1,0:T(8,128)} %copy-done.46), kind=kOutput, calls=%fused_computation.90 | convolution fusion | flops 4304928768 | bytes 22020096 | tf_op jit(solution)/shard_map/dot_general | solution.py:20
  195.7 6.8 reduce-scatter.17.cloned.1.call-done
  206.7 18.2 %reduce-scatter.15.cloned.1.call-done = bf16[128,2048]{1,0:T(8,128)(2,1)} async-done(((bf16[256,2048]{1,0:T(8,128)(2,1)}), bf16[128,2048]{1,0:T(8,128)(2,1)}) %reduce-scatter.15.cloned.1.call-update) | async-done | bytes 524304 | tf_op jit(solution)/shard_map/reduce_scatter | solution.py:144
  224.9 3.2 fusion.89
  230.6 20.8 %all-gather.11.cloned.1.call-done = bf16[256,2048]{1,0:T(8,128)(2,1)} async-done(((bf16[128,2048]{1,0:T(8,128)(2,1)}), bf16[256,2048]{1,0:T(8,128)(2,1)}) %all-gather.11.cloned.1.call-update) | async-done | bytes 1048592 | tf_op jit(solution)/shard_map/all_gather | solution.py:170
  251.4 3.8 convolution_convert_fusion.6
  260.7 32.3 %while.52 = (s32[]{:T(128)}, f32[256,8,128]{0,2,1:T(8,128)}, f32[1024,8,128]{2,0,1:T(8,128)}, f32[1024,8,128]{2,0,1:T(8,128)}, bf16[1024,8,128]{2,0,1:T(8,128)(2...) while((s32[]{:T(128)}, f32[256,8,128]{0,2,1:T(8,128)}, ...), condition=%wide.region_17.18_spmd.clone, body=%wide.region_16.17_spmd.clone.sunk | while | flops 1356727040 | bytes 111452632 | solution.py:215
  261.1 3.0 fusion.167
  269.9 3.9 fusion.170
  282.9 3.3 fusion.169
  286.2 3.9 fusion.170
  293.0 3.8 convert_element_type.252
  296.9 4.0 convert_element_type.251
  301.7 26.7 %reduce-scatter.21.cloned.1.call-done = bf16[256,8,128]{2,0,1:T(8,128)(2,1)} async-done(((bf16[1024,8,128]{2,0,1:T(8,128)(2,1)}), bf16[256,8,128]{2,0,1:T(8,128)(2,1)}) %reduce-scatter.21.cloned.1.call-update) | async-done | bytes 524304 | tf_op jit(solution)/shard_map/reduce_scatter | solution.py:222
  330.1 32.4 %reduce-scatter.19.cloned.1.call-done = bf16[256,8,128]{2,0,1:T(8,128)(2,1)} async-done(((bf16[1024,8,128]{2,0,1:T(8,128)(2,1)}), bf16[256,8,128]{2,0,1:T(8,128)(2,1)}) %reduce-scatter.19.cloned.1.call-update) | async-done | bytes 524304 | tf_op jit(solution)/shard_map/reduce_scatter | solution.py:219
  364.8 9.3 fusion.60
  378.4 16.2 %reduce-scatter.23.cloned.1.call-done = bf16[128,2048]{1,0:T(8,128)(2,1)} async-done(((bf16[256,2048]{1,0:T(8,128)(2,1)}), bf16[128,2048]{1,0:T(8,128)(2,1)}) %reduce-scatter.23.cloned.1.call-update) | async-done | bytes 524304 | tf_op jit(solution)/shard_map/reduce_scatter | solution.py:238
  398.9 4.3 convolution_convert_fusion.2
  403.3 49.7 %all-reduce.5.cloned.1.call-done = (f32[2048]{0:T(1024)}, f32[2048]{0:T(1024)}, f32[2,2048]{1,0:T(2,128)}, f32[2048]{0:T(1024)}, f32[2048]{0:T(1024)}, /*index=5*/f32[2048]{0:T(1024)}, f32[8192]{0:T(1024)}, f32[2048]{0:T(1024)}) async-done(((f32[2048]{0:T(1024)}, f32[2048]{0:T(1024)}, f32[2,2048]{1,0:T(2,128)}, f32[2048]{0:T(1024)}, f32[2048]{0:T(1024)}, /*index=5*/f32[2048]{0:T(1024)}, f32[8192]{0:T(1024)}, ...) | async-done | bytes 98320 | tf_op jit(solution)/shard_map/psum | solution.py:282
  453.1 11.5 %convert_bitcast_fusion = bf16[2048,4096]{0,1:T(8,128)(2,1)} fusion(bf16[1,256,2048]{2,1,0:T(8,128)(2,1)S(1)} %copy-done.22, f32[256,4096]{1,0:T(8,128)} %copy-done.46), kind=kOutput, calls=%fused_computation.72 | convolution fusion | flops 4312793088 | bytes 22020096 | tf_op jit(solution)/shard_map/dot_general | solution.py:20
  464.6 21.7 %copy.68 = bf16[2048,4096]{1,0:T(8,128)(2,1)} copy(bf16[2048,4096]{0,1:T(8,128)(2,1)} %convert_bitcast_fusion) | data formatting | bytes 33554432
  487.7 9.8 convolution_convert_fusion
  498.7 8.0 convolution_convert_fusion.1
  506.7 23.5 %reduce-scatter.27.cloned.1.call-done = bf16[128,1024]{1,0:T(8,128)(2,1)} async-done(((bf16[2048,1024]{1,0:T(8,128)(2,1)}), bf16[128,1024]{1,0:T(8,128)(2,1)}) %reduce-scatter.27.cloned.1.call-update) | async-done | bytes 262160 | tf_op jit(solution)/shard_map/reduce_scatter | solution.py:253
  534.3 32.9 %all-reduce.7.cloned.1.call-done = (f32[2048]{0:T(1024)}, f32[2048]{0:T(1024)}, f32[2,2048]{1,0:T(2,128)}, f32[2048]{0:T(1024)}, f32[2048]{0:T(1024)}, /*index=5*/f32[2048]{0:T(1024)}, f32[8192]{0:T(1024)}, f32[2048]{0:T(1024)}) async-done(((f32[2048]{0:T(1024)}, f32[2048]{0:T(1024)}, f32[2,2048]{1,0:T(2,128)}, f32[2048]{0:T(1024)}, f32[2048]{0:T(1024)}, /*index=5*/f32[2048]{0:T(1024)}, f32[8192]{0:T(1024)}, ...) | async-done | bytes 98320 | tf_op jit(solution)/shard_map/psum | solution.py:282
  569.8 180.3 %reduce-scatter.31.cloned.1.call-done = bf16[128,4096]{1,0:T(8,128)(2,1)} async-done(((bf16[2048,4096]{1,0:T(8,128)(2,1)}), bf16[128,4096]{1,0:T(8,128)(2,1)}) %reduce-scatter.31.cloned.1.call-update) | async-done | bytes 1048592
  753.5 178.8 %reduce-scatter.29.cloned.1.call-done = bf16[128,4096]{1,0:T(8,128)(2,1)} async-done(((bf16[2048,4096]{1,0:T(8,128)(2,1)}), bf16[128,4096]{1,0:T(8,128)(2,1)}) %reduce-scatter.29.cloned.1.call-update) | async-done | bytes 1048592 | tf_op jit(solution)/shard_map/reduce_scatter | solution.py:256
  935.1 135.3 %reduce-scatter.25.cloned.1.call-done = bf16[128,3,1024]{2,0,1:T(8,128)(2,1)} async-done(((bf16[2048,3,1024]{2,0,1:T(8,128)(2,1)}), bf16[128,3,1024]{2,0,1:T(8,128)(2,1)}) %reduce-scatter.25.cloned.1.call-update) | async-done | bytes 786448 | tf_op jit(solution)/shard_map/reduce_scatter | solution.py:250
  (266 shorter events, 89.0 us)
Async XLA Ops:
  7.2 39.8 %all-gather.7.cloned.1.call-start = ((), (), s32[]{:S(2)}) async-start(), calls=%async_computation.11 | async-start | bytes 2621440 | tf_op jit(solution)/shard_map/all_gather | solution.py:75
  7.9 10.8 copy-start.30
  8.6 10.1 copy-start.24
  10.1 8.7 copy-start.42
  11.7 7.0 copy-start.44
  21.5 50.2 %all-gather.5.cloned.1.call-start = ((), (), s32[]{:S(2)}) async-start(), calls=%async_computation.10 | async-start | bytes 2621440 | tf_op jit(solution)/shard_map/all_gather | solution.py:76
  24.6 100.1 %reduce-scatter.13.cloned.1.call-start = ((), (), s32[]{:S(2)}) async-start(), calls=%async_computation.12 | async-start | bytes 1572864 | tf_op jit(solution)/shard_map/reduce_scatter | solution.py:130
  99.5 5.2 copy-start.38
  99.5 5.2 copy-start.39
  99.5 5.3 copy-start.40
  104.3 23.1 %copy-start.29 = (bf16[4096]{0:T(1024)(128)(2,1)S(1)}, bf16[4096]{0:T(1024)(128)(2,1)}, u32[]{:S(2)}) copy-start(bf16[4096]{0:T(1024)(128)(2,1)} %param.32) | copy-start | bytes 24580
  104.3 44.5 %all-gather.9.cloned.1.call-start = ((), (), s32[]{:S(2)}) async-start(), calls=%async_computation.13 | async-start | bytes 1572864 | tf_op jit(solution)/shard_map/all_gather | solution.py:138
  104.7 52.6 %copy-start.7 = (f32[1,256,2048]{2,1,0:T(8,128)}, f32[1,256,2048]{2,1,0:T(8,128)S(1)}, u32[]{:S(2)}) copy-start(f32[1,256,2048]{2,1,0:T(8,128)S(1)} %convert_element_type.219) | copy-start | bytes 6291460
  127.3 75.1 %reduce-scatter.17.cloned.1.call-start = ((), (), s32[]{:S(2)}) async-start(), calls=%async_computation.15 | async-start | bytes 1572864 | tf_op jit(solution)/shard_map/reduce_scatter | solution.py:161
  148.8 8.5 copy-start.20
  157.3 12.7 %copy-start.46 = (f32[256,4096]{1,0:T(8,128)}, f32[256,4096]{1,0:T(8,128)S(1)}, u32[]{:S(2)}) copy-start(f32[256,4096]{1,0:T(8,128)S(1)} %convolution_add_fusion) | copy-start | bytes 12582916
  182.0 13.7 %copy-start.41 = (bf16[2048]{0:T(1024)(128)(2,1)S(1)}, bf16[2048]{0:T(1024)(128)(2,1)}, u32[]{:S(2)}) copy-start(bf16[2048]{0:T(1024)(128)(2,1)} %param.34) | copy-start | bytes 12292
  182.0 42.9 %reduce-scatter.15.cloned.1.call-start = ((), (), s32[]{:S(2)}) async-start(), calls=%async_computation.14 | async-start | bytes 1572864 | tf_op jit(solution)/shard_map/reduce_scatter | solution.py:144
  195.6 29.3 %copy-start.21 = (bf16[1,256,2048]{2,1,0:T(8,128)(2,1)S(1)}, bf16[1,256,2048]{2,1,0:T(8,128)(2,1)}, u32[]{:S(2)}) copy-start(bf16[1,256,2048]{2,1,0:T(8,128)(2,1)} %param.35) | copy-start | bytes 3145732
  195.6 55.8 %all-gather.11.cloned.1.call-start = ((), (), s32[]{:S(2)}) async-start(), calls=%async_computation.16 | async-start | bytes 1572864 | tf_op jit(solution)/shard_map/all_gather | solution.py:170
  204.5 25.8 %copy-start.13 = (f32[256,8,128]{0,2,1:T(8,128)S(1)}, f32[256,8,128]{0,2,1:T(8,128)}, u32[]{:S(2)}) copy-start(f32[256,8,128]{0,2,1:T(8,128)} %get-tuple-element.946) | copy-start | bytes 3145732
  229.9 98.5 %reduce-scatter.21.cloned.1.call-start = ((), (), s32[]{:S(2)}) async-start(), calls=%async_computation.18 | async-start | bytes 2621440 | tf_op jit(solution)/shard_map/reduce_scatter | solution.py:222
  261.1 5.0 copy-start.3
  266.9 6.9 copy-start.4
  282.9 7.2 copy-start.4
  296.9 65.5 %reduce-scatter.19.cloned.1.call-start = ((), (), s32[]{:S(2)}) async-start(), calls=%async_computation.17 | async-start | bytes 2621440 | tf_op jit(solution)/shard_map/reduce_scatter | solution.py:219
  300.9 93.7 %reduce-scatter.23.cloned.1.call-start = ((), (), s32[]{:S(2)}) async-start(), calls=%async_computation.19 | async-start | bytes 1572864 | tf_op jit(solution)/shard_map/reduce_scatter | solution.py:238
  301.7 72.4 %copy-start.17 = (bf16[256,1,1024]{2,0,1:T(8,128)(2,1)}, bf16[256,1,1024]{2,0,1:T(8,128)(2,1)S(1)}, u32[]{:S(2)}) copy-start(bf16[256,1,1024]{2,0,1:T(8,128)(2,1)S(1)} %copy.66) | copy-start | bytes 1572868
  330.0 44.1 %copy-start.18 = (bf16[256,1,1024]{2,0,1:T(8,128)(2,1)}, bf16[256,1,1024]{2,0,1:T(8,128)(2,1)S(1)}, u32[]{:S(2)}) copy-start(bf16[256,1,1024]{2,0,1:T(8,128)(2,1)S(1)} %stack_reshape.14) | copy-start | bytes 1572868
  364.8 9.4 copy-start.8
  374.1 20.5 %copy-start.25 = (f32[2048]{0:T(1024)S(1)}, f32[2048]{0:T(1024)}, u32[]{:S(2)}) copy-start(f32[2048]{0:T(1024)} %copy-done.24) | copy-start | bytes 24580
  374.1 78.9 %all-reduce.5.cloned.1.call-start = ((), (), s32[]{:S(2)}) async-start(), calls=%async_computation.24 | async-start | bytes 196608 | tf_op jit(solution)/shard_map/psum | solution.py:282
  374.4 24.6 %copy-start.14 = (bf16[256,2048]{1,0:T(8,128)(2,1)S(1)}, bf16[256,2048]{1,0:T(8,128)(2,1)}, u32[]{:S(2)}) copy-start(bf16[256,2048]{1,0:T(8,128)(2,1)} %all-gather.11.cloned.1.call-done) | copy-start | bytes 3145732
  376.6 22.3 %copy-start.26 = (f32[8192]{0:T(1024)}, f32[8192]{0:T(1024)S(1)}, u32[]{:S(2)}) copy-start(f32[8192]{0:T(1024)S(1)} %dynamic_update_slice.21) | copy-start | bytes 98308
  378.4 20.5 %copy-start.27 = (f32[2,2048]{1,0:T(2,128)}, f32[2,2048]{1,0:T(2,128)S(1)}, u32[]{:S(2)}) copy-start(f32[2,2048]{1,0:T(2,128)S(1)} %constant_dynamic-update-slice_fusion) | copy-start | bytes 49156
  398.9 131.4 %reduce-scatter.27.cloned.1.call-start = ((), (), s32[]{:S(2)}) async-start(), calls=%async_computation.21 | async-start | bytes 4456448 | tf_op jit(solution)/shard_map/reduce_scatter | solution.py:253
  403.2 49.9 %copy-start.22 = (bf16[1,256,2048]{2,1,0:T(8,128)(2,1)S(1)}, bf16[1,256,2048]{2,1,0:T(8,128)(2,1)}, u32[]{:S(2)}) copy-start(bf16[1,256,2048]{2,1,0:T(8,128)(2,1)} %param.35) | copy-start | bytes 3145732
  403.3 163.9 %all-reduce.7.cloned.1.call-start = ((), (), s32[]{:S(2)}) async-start(), calls=%async_computation.25 | async-start | bytes 196608 | tf_op jit(solution)/shard_map/psum | solution.py:282
  453.0 297.1 %reduce-scatter.31.cloned.1.call-start = ((), (), s32[]{:S(2)}) async-start(), calls=%async_computation.23 | async-start | bytes 17825792
  486.3 446.0 %reduce-scatter.29.cloned.1.call-start = ((), (), s32[]{:S(2)}) async-start(), calls=%async_computation.22 | async-start | bytes 17825792 | tf_op jit(solution)/shard_map/reduce_scatter | solution.py:256
  497.5 572.9 %reduce-scatter.25.cloned.1.call-start = ((), (), s32[]{:S(2)}) async-start(), calls=%async_computation.20 | async-start | bytes 13369344 | tf_op jit(solution)/shard_map/reduce_scatter | solution.py:250
  506.7 25.4 %copy-start.12 = (f32[128,2048]{1,0:T(8,128)S(1)}, f32[128,2048]{1,0:T(8,128)}, u32[]{:S(2)}) copy-start(f32[128,2048]{1,0:T(8,128)} %copy-done.11) | copy-start | bytes 3145732
  751.8 321.1 %copy-start.37 = (f32[2048]{0:T(1024)S(1)}, f32[2048]{0:T(1024)}, u32[]{:S(2)}) copy-start(f32[2048]{0:T(1024)} %get-tuple-element.1328) | copy-start | bytes 24580
  751.8 321.7 %copy-start.36 = (f32[2048]{0:T(1024)S(1)}, f32[2048]{0:T(1024)}, u32[]{:S(2)}) copy-start(f32[2048]{0:T(1024)} %get-tuple-element.1329) | copy-start | bytes 24580
  751.8 322.2 %copy-start.35 = (f32[2048]{0:T(1024)S(1)}, f32[2048]{0:T(1024)}, u32[]{:S(2)}) copy-start(f32[2048]{0:T(1024)} %get-tuple-element.1333) | copy-start | bytes 24580
  751.8 322.8 %copy-start.34 = (f32[2048]{0:T(1024)S(1)}, f32[2048]{0:T(1024)}, u32[]{:S(2)}) copy-start(f32[2048]{0:T(1024)} %get-tuple-element.1334) | copy-start | bytes 24580
  751.8 323.4 %copy-start.33 = (f32[2048]{0:T(1024)S(1)}, f32[2048]{0:T(1024)}, u32[]{:S(2)}) copy-start(f32[2048]{0:T(1024)} %get-tuple-element.1335) | copy-start | bytes 24580
  751.8 324.0 %copy-start.32 = (f32[2048]{0:T(1024)S(1)}, f32[2048]{0:T(1024)}, u32[]{:S(2)}) copy-start(f32[2048]{0:T(1024)} %get-tuple-element.1339) | copy-start | bytes 24580
  (21 other events, 54.4 us)
Sparse Core Ops, SparseCore 0:
  21.7 25.2 all-gather.6
  49.1 22.5 all-gather.4
  104.4 20.2 reduce-scatter.12
  127.4 21.3 all-gather.8
  182.1 20.3 reduce-scatter.16
  204.5 20.3 reduce-scatter.14
  230.1 21.2 all-gather.10
  297.0 31.3 reduce-scatter.20
  331.0 31.4 reduce-scatter.18
  374.3 20.3 reduce-scatter.22
  399.7 53.2 all-reduce.4
  457.2 72.9 reduce-scatter.26
  533.1 34.0 all-reduce.6
  571.7 178.3 reduce-scatter.30
  754.7 177.5 reduce-scatter.28
  936.7 133.5 reduce-scatter.24
